TPU v7x, 256 devices: a whole 4x4x8 slice. The times are simulated.
256 devices in a mesh: group: 16 (over z, core), shard: 16 (over y, x).
Axes of the slice: x: 4, y: 4, z: 8, core: 2. Of those that a mesh axis runs over, the one named last changes fastest.
Arguments:
- tokens: bfloat16 [512, 1280], P(('group', 'shard')), as said below
- kv_cache: bfloat16 [512, 128, 2560], P(('group', 'shard'))
- keep_list: int32 [512, 128], P(('group', 'shard')), may hold values from 0 to 1
- lengths: int32 [512], P(('group', 'shard')), may hold values from 64 to 128
- merge_index: int32 [512, 128], P(('group', 'shard')), may hold values from 0 to 15
- merge_table: bfloat16 [16], replicated, may hold values from 0.0099487305 to 0.099609375
- move_offset: int32 [16, 2], P('shard'), may hold values from 0 to 15, as said below
- pair_mask: int32 [16], P('shard'), may hold values from 1 to 15
- w_qkv: bfloat16 [1280, 3840], P(None, 'shard'), may hold values from -0.15625 to 0.15625
- w_out: bfloat16 [1280, 1280], P(None, 'shard'), may hold values from -0.15625 to 0.15625
- w_up: bfloat16 [1280, 5120], P(None, 'shard'), may hold values from -0.15625 to 0.15625
- w_gate: bfloat16 [1280, 5120], P(None, 'shard'), may hold values from -0.15625 to 0.15625
- w_down: bfloat16 [5120, 1280], P('shard'), may hold values from -0.078125 to 0.078125
- qk_scale: float32 [1280], replicated, may hold values from 0.5 to 2
- attn_rate: float32 [1280], replicated, may hold values from 0.05 to 0.5
- mlp_rate: float32 [1280], replicated, may hold values from 0.05 to 0.5
- up_scale: float32 [5120], P('shard'), may hold values from 0.5 to 2
- gate_scale: float32 [5120], P('shard'), may hold values from 0.5 to 2
Outputs:
- new_hidden: bfloat16 [512, 1280], P(('group', 'shard'))
- moved_cache: bfloat16 [512, 128, 2560], P(('group', 'shard'))
Inputs may be any that keep to these rules, and one draw needn't show every extreme that they name: `tokens`: slot 1 of group g and shard s holds the same token as that slot of group g XOR pair_mask[s] on shard s. `move_offset`: the 2 offsets of one shard index are distinct.
All inputs are finite; a program needn't handle non-finite values.
Results may differ from a plain program's by a relative error of at most 0.011.
Values may be sent and summed in bfloat16 or wider, within the bound.
A program may use at most 128 MiB of HBM per device.

v0:
```python
import jax
import jax.numpy as jnp
from jax import lax
from jax.sharding import PartitionSpec as P

DH = 64
BLOCK = 128
WTAB = 16
EPSILON = 1e-06
NEGATIVE = -1e30


def rms_normal(vector):
    return vector * lax.rsqrt(jnp.mean(vector * vector, axis=-1, keepdims=True) + EPSILON)


def head_normal(vector, scaling):
    return vector * lax.rsqrt(jnp.sum(vector * vector, axis=-1, keepdims=True) + EPSILON) * scaling


def rounded(vector):
    return lax.optimization_barrier(vector.astype(jnp.bfloat16)).astype(jnp.float32)


def spread_columns(row_block, weight):
    columns = jnp.dot(
        lax.all_gather(row_block, "shard", axis=0, tiled=True),
        weight,
        preferred_element_type=jnp.float32,
    ).astype(jnp.bfloat16)
    return lax.all_to_all(columns, "shard", split_axis=0, concat_axis=1, tiled=True)


def compact_local(kv_cache, keep_list, lengths, merge_index, merge_table):
    slot_count, context, doubled = kv_cache.shape
    block_count = context // BLOCK
    in_length = jnp.arange(context, dtype=jnp.int32)[None, :] < lengths[:, None]
    keeper = (keep_list == 1) & in_length
    dropper = (keep_list == 0) & in_length
    position = jnp.cumsum(keeper.astype(jnp.int32), axis=1) - 1
    kept_count = jnp.sum(keeper.astype(jnp.int32), axis=1)
    drop_count = jnp.sum(dropper.astype(jnp.int32), axis=1)
    table_hits = merge_index[:, :, None] == jnp.arange(WTAB, dtype=jnp.int32)[None, None, :]
    weights = jnp.sum(
        jnp.where(table_hits, merge_table.astype(jnp.float32)[None, None, :], 0.0), axis=2
    ) * dropper.astype(jnp.float32)
    target = jnp.arange(BLOCK, dtype=jnp.int32)
    placing = (position[:, None, :] == target[None, :, None]) & keeper[:, None, :]
    summing = jnp.where(
        target[None, :, None] == kept_count[:, None, None], weights[:, None, :], 0.0
    )
    mixing = (placing.astype(jnp.float32) + summing).astype(jnp.bfloat16)
    packed = jnp.einsum(
        "ndk,nkc->ndc", mixing, kv_cache, preferred_element_type=jnp.float32
    ).astype(jnp.bfloat16)
    live_count = (kept_count + (drop_count > 0).astype(jnp.int32)).reshape(slot_count, block_count)
    return (packed, live_count.astype(jnp.bfloat16))


def per_device(
    tokens,
    kv_cache,
    keep_list,
    lengths,
    merge_index,
    merge_table,
    move_offset,
    pair_mask,
    w_qkv,
    w_out,
    w_up,
    w_gate,
    w_down,
    qk_scale,
    attn_rate,
    mlp_rate,
    up_scale,
    gate_scale,
):
    slot_count, context, doubled = kv_cache.shape
    model_width = tokens.shape[1]
    head_count = model_width // DH
    group_count = lax.axis_size("group")
    group_index = lax.axis_index("group")
    packed, live_count = compact_local(kv_cache, keep_list, lengths, merge_index, merge_table)
    offsets = move_offset[0]
    target = (group_index + offsets) % group_count
    sender = (jnp.arange(group_count, dtype=jnp.int32)[:, None] == target[None, :]).astype(
        jnp.bfloat16
    )
    outgoing = jnp.einsum("pj,jrc->prc", sender, packed, preferred_element_type=jnp.float32).astype(
        jnp.bfloat16
    )
    outgoing_live = jnp.einsum(
        "pj,jb->pb", sender, live_count, preferred_element_type=jnp.float32
    ).astype(jnp.bfloat16)
    incoming, incoming_live = (
        lax.all_to_all(outgoing, "group", split_axis=0, concat_axis=0, tiled=True),
        lax.all_to_all(outgoing_live, "group", split_axis=0, concat_axis=0, tiled=True),
    )
    source = (group_index - offsets) % group_count
    picker = (source[:, None] == jnp.arange(group_count, dtype=jnp.int32)[None, :]).astype(
        jnp.bfloat16
    )
    moved_cache = jnp.einsum(
        "jp,prc->jrc", picker, incoming, preferred_element_type=jnp.float32
    ).astype(jnp.bfloat16)
    moved_live = jnp.einsum("jp,pb->jb", picker, incoming_live, preferred_element_type=jnp.float32)
    projected = spread_columns(tokens, w_qkv)
    head_scale = qk_scale.reshape(head_count, DH)
    queries = head_normal(
        projected[:, :model_width].astype(jnp.float32).reshape(slot_count, head_count, DH),
        head_scale,
    ).astype(jnp.bfloat16)
    new_keys = head_normal(
        projected[:, model_width : 2 * model_width]
        .astype(jnp.float32)
        .reshape(slot_count, head_count, DH),
        head_scale,
    ).astype(jnp.bfloat16)
    new_values = projected[:, 2 * model_width :].reshape(slot_count, head_count, DH)
    key_rows = moved_cache[:, :, :model_width].reshape(slot_count, context, head_count, DH)
    value_rows = moved_cache[:, :, model_width:].reshape(slot_count, context, head_count, DH)
    score_scale = float(DH) ** 0.5
    scores = score_scale * jnp.einsum(
        "jhd,jrhd->jhr", queries, key_rows, preferred_element_type=jnp.float32
    )
    fresh_score = score_scale * jnp.sum(
        queries.astype(jnp.float32) * new_keys.astype(jnp.float32), axis=-1
    )
    row_valid = (jnp.arange(context, dtype=jnp.int32) % BLOCK).astype(jnp.float32)[
        None, :
    ] < jnp.repeat(moved_live, BLOCK, axis=1)
    pair_bits = pair_mask[0]
    partner = jnp.bitwise_xor(group_index, pair_bits)
    with_new = (jnp.arange(slot_count, dtype=jnp.int32) < slot_count - 1) | (group_index < partner)
    highest = jnp.maximum(
        jnp.max(jnp.where(row_valid[:, None, :], scores, NEGATIVE), axis=2),
        jnp.where(with_new[:, None], fresh_score, NEGATIVE),
    )
    safe_scores = jnp.where(row_valid[:, None, :], scores, highest[:, :, None])
    soft_weights = jnp.where(row_valid[:, None, :], jnp.exp(safe_scores - highest[:, :, None]), 0.0)
    fresh_weight = jnp.where(with_new[:, None], jnp.exp(fresh_score - highest), 0.0)
    weight_sum = jnp.sum(soft_weights, axis=2) + fresh_weight
    weighted = jnp.einsum(
        "jhr,jrhd->jhd",
        soft_weights.astype(jnp.bfloat16),
        value_rows,
        preferred_element_type=jnp.float32,
    )
    weighted = weighted + rounded(fresh_weight)[:, :, None] * new_values.astype(jnp.float32)
    last_high = highest[slot_count - 1 :]
    last_sum = weight_sum[slot_count - 1 :]
    last_weighted = weighted[slot_count - 1 :]
    gathered_high, gathered_sum, gathered_weighted = (
        lax.all_gather(last_high, "group", axis=0, tiled=True),
        lax.all_gather(last_sum, "group", axis=0, tiled=True),
        lax.all_gather(last_weighted, "group", axis=0, tiled=True),
    )
    picker_group = (jnp.arange(group_count, dtype=jnp.int32) == partner).astype(jnp.float32)
    other_high = jnp.sum(picker_group[:, None] * gathered_high, axis=0, keepdims=True)
    other_sum = jnp.sum(picker_group[:, None] * gathered_sum, axis=0, keepdims=True)
    other_weighted = jnp.sum(picker_group[:, None, None] * gathered_weighted, axis=0, keepdims=True)
    merged = jnp.maximum(last_high, other_high)
    own_factor = jnp.exp(last_high - merged)
    other_factor = jnp.exp(other_high - merged)
    long_sum = last_sum * own_factor + other_sum * other_factor
    long_weighted = (
        last_weighted * own_factor[:, :, None] + other_weighted * other_factor[:, :, None]
    )
    weight_sum = jnp.concatenate([weight_sum[: slot_count - 1], long_sum], axis=0)
    weighted = jnp.concatenate([weighted[: slot_count - 1], long_weighted], axis=0)
    attended = (
        (weighted / weight_sum[:, :, None]).reshape(slot_count, model_width).astype(jnp.bfloat16)
    )
    attention_out = spread_columns(attended, w_out)
    hidden = tokens.astype(jnp.float32)
    mixed = rms_normal(
        hidden + attn_rate * (rms_normal(attention_out.astype(jnp.float32)) - hidden)
    )
    mixed_low = mixed.astype(jnp.bfloat16)
    gate_factor = gate_scale * float(model_width) ** 0.5
    shard_rows = lax.all_gather(mixed_low, "shard", axis=0, tiled=True)
    up_part = jnp.dot(shard_rows, w_up, preferred_element_type=jnp.float32) * up_scale
    gate_part = jnp.dot(shard_rows, w_gate, preferred_element_type=jnp.float32) * gate_factor
    inner = (up_part * jax.nn.silu(gate_part)).astype(jnp.bfloat16)
    partial_terms = jnp.dot(inner, w_down, preferred_element_type=jnp.float32)
    mlp_out = lax.psum_scatter(
        partial_terms.astype(jnp.bfloat16), "shard", scatter_dimension=0, tiled=True
    ).astype(jnp.float32)
    new_hidden = rms_normal(mixed + mlp_rate * (rms_normal(mlp_out) - mixed)).astype(jnp.bfloat16)
    return (new_hidden, moved_cache)


def solution(mesh):
    return jax.shard_map(
        per_device,
        mesh=mesh,
        in_specs=(
            P(("group", "shard"), None),
            P(("group", "shard"), None, None),
            P(("group", "shard"), None),
            P(("group", "shard")),
            P(("group", "shard"), None),
            P(),
            P("shard", None),
            P("shard"),
            P(None, "shard"),
            P(None, "shard"),
            P(None, "shard"),
            P(None, "shard"),
            P("shard", None),
            P(),
            P(),
            P(),
            P("shard"),
            P("shard"),
        ),
        out_specs=(P(("group", "shard"), None), P(("group", "shard"), None, None)),
        check_vma=False,
    )
```

profile of v0, /device:TPU:32, one launch (start us, length us, event | category | flops | bytes accessed | tf_op | source)
XLA Modules:
  0.0 549.3 jit_solution(16223864282160331246)
XLA Ops:
  7.2 0.8 convert_element_type.140
  7.9 0.8 select_reduce_fusion.1
  8.7 0.8 fusion.64
  9.5 0.8 broadcast_select_fusion
  10.2 0.7 fusion.43
  10.9 0.1 convert_reduce_fusion
  11.1 0.2 fusion.9
  11.2 0.7 copy.91
  11.9 8.6 %all-to-all-start = ((bf16[16,1,1]{2,1,0:T(2,128)(2,1)}), bf16[16,1,1]{2,1,0:T(2,128)(2,1)S(1)}, u32[]{:S(2)}, u32[]{:S(2)}) async-start(bf16[16,1,1]{2,1,0:T(2,128)(2,1)} %copy.91), calls=%async_computation | async-start | bytes 16384 | tf_op jit(solution)/shard_map/all_to_all | solution.py:99
  20.6 0.3 reduce_window_sum.11
  20.9 23.9 %all-gather = bf16[16,2,1280]{2,1,0:T(2,128)(2,1)S(1)} all-gather(bf16[1,2,1280]{2,1,0:T(2,128)(2,1)} %bitcast.99), channel_id=1, replica_groups=mesh['group'=16,'shard'=16] {'shard'}, dimensions={0}, use_global_device_ids=true | all-gather | bytes 87040 | tf_op jit(solution)/shard_map/all_gather | solution.py:27
  44.9 1.3 convolution_convert_fusion.3
  46.2 0.6 convolution_convert_fusion.1
  46.8 0.6 all_to_all.35
  47.5 4.7 all-to-all-start.1
  52.1 6.1 %convolution_convert_fusion = bf16[16,128,2560]{2,0,1:T(8,128)(2,1)} fusion(bf16[2,128,2560]{2,1,0:T(8,128)(2,1)S(1)} %convolution_convert_fusion.1, s32[2]{0:T(128)S(1)} %fusion.43), kind=kOutput, calls=%fused_computation.2 | convolution fusion | flops 26214432 | bytes 11796488 | tf_op jit(solution)/shard_map/pj,jrc->prc/dot_general | solution.py:91
  58.2 13.7 %copy.94 = bf16[16,128,2560]{2,1,0:T(8,128)(2,1)} copy(bf16[16,128,2560]{2,0,1:T(8,128)(2,1)} %convolution_convert_fusion) | data formatting | bytes 20971520 | tf_op jit(solution)/shard_map/convert_element_type | solution.py:91
  72.0 7.4 %all-to-all-start.2 = ((bf16[16,128,2560]{2,1,0:T(8,128)(2,1)}), bf16[16,128,2560]{2,1,0:T(8,128)(2,1)}, u32[]{:S(2)}, u32[]{:S(2)}) async-start(bf16[16,128,2560]{2,1,0:T(8,128)(2,1)} %copy.94), calls=%async_computation.2 | async-start | bytes 20971520 | tf_op jit(solution)/shard_map/all_to_all | solution.py:98
  80.1 0.2 reduce.2
  80.3 0.2 convolution_bitcast_fusion
  81.2 0.2 multiply_reduce_fusion.1
  81.4 225.6 %all-to-all-done.2 = bf16[16,128,2560]{2,1,0:T(8,128)(2,1)} async-done(((bf16[16,128,2560]{2,1,0:T(8,128)(2,1)}), bf16[16,128,2560]{2,1,0:T(8,128)(2,1)}, u32[]{:S(2)}, u32[]{:S(2)}) %all-to-all-start.2) | async-done | bytes 10485792 | tf_op jit(solution)/shard_map/all_to_all | solution.py:98
  306.9 15.7 %fusion.2 = bf16[2,128,2560]{2,0,1:T(2,128)(2,1)S(1)} fusion(bf16[16,128,2560]{2,1,0:T(8,128)(2,1)} %all-to-all-done.2, s32[2]{0:T(128)S(1)} %and_select_fusion.1), kind=kOutput, calls=%fused_computation.3 | convolution fusion | flops 21626912 | bytes 11796488 | tf_op jit(solution)/shard_map/jp,prc->jrc/dot_general | solution.py:105
  322.7 1.7 fusion.65
  324.4 3.0 copy.96
  327.3 1.4 fusion.25
  329.1 15.7 %all-gather.1 = f32[16,1,20]{2,1,0:T(1,128)S(1)} all-gather(f32[1,1,20]{2,1,0:T(1,128)S(1)} %slice_bitcast_fusion.1), channel_id=1, replica_groups=mesh['group'=16,'shard'=16] {'group'}, dimensions={0}, use_global_device_ids=true | all-gather | bytes 1360 | tf_op jit(solution)/shard_map/all_gather | solution.py:156
  345.1 15.6 %all-gather.2 = f32[16,1,20]{2,1,0:T(1,128)S(1)} all-gather(f32[1,1,20]{2,1,0:T(1,128)S(1)} %slice_bitcast_fusion), channel_id=1, replica_groups=mesh['group'=16,'shard'=16] {'group'}, dimensions={0}, use_global_device_ids=true | all-gather | bytes 1360 | tf_op jit(solution)/shard_map/all_gather | solution.py:157
  361.0 1.9 copy.99
  362.9 1.5 fusion.23
  364.5 15.2 %all_gather.20 = f32[16,20,64]{2,1,0:T(8,128)S(1)} all-gather(f32[1,20,64]{2,1,0:T(8,128)S(1)} %slice.46), channel_id=1, replica_groups=mesh['group'=16,'shard'=16] {'group'}, dimensions={0}, use_global_device_ids=true | all-gather | bytes 87040 | tf_op jit(solution)/shard_map/all_gather | solution.py:158
  380.1 25.8 %all-gather.3 = bf16[16,2,1280]{2,1,0:T(2,128)(2,1)} all-gather(bf16[1,2,1280]{2,1,0:T(2,128)(2,1)S(1)} %fusion.36), channel_id=1, replica_groups=mesh['group'=16,'shard'=16] {'shard'}, dimensions={0}, use_global_device_ids=true | all-gather | bytes 87040 | tf_op jit(solution)/shard_map/all_gather | solution.py:27
  405.9 0.9 reshape.284
  406.8 1.7 convolution_convert_fusion.4
  408.6 4.6 all-to-all-start.3
  413.2 7.4 %all-to-all-done.3 = bf16[16,2,80]{2,1,0:T(2,128)(2,1)S(1)} async-done(((bf16[16,2,80]{2,1,0:T(2,128)(2,1)}), bf16[16,2,80]{2,1,0:T(2,128)(2,1)S(1)}, u32[]{:S(2)}, u32[]{:S(2)}) %all-to-all-start.3) | async-done | bytes 5152 | tf_op jit(solution)/shard_map/all_to_all | solution.py:31
  420.7 0.1 fusion.27
  420.9 0.2 multiply_reduce_fusion.5
  421.2 23.5 %all-gather.4 = bf16[16,2,1280]{2,1,0:T(2,128)(2,1)} all-gather(bf16[1,2,1280]{2,1,0:T(2,128)(2,1)S(1)} %fusion.35), channel_id=1, replica_groups=mesh['group'=16,'shard'=16] {'shard'}, dimensions={0}, use_global_device_ids=true | all-gather | bytes 87040 | tf_op jit(solution)/shard_map/all_gather | solution.py:183
  444.6 0.9 reshape.286
  445.6 2.1 convolution_multiply_fusion
  447.7 2.6 convolution_convert_fusion.2
  450.3 0.6 dynamic-slice
  451.5 1.2 copy.102
  452.7 87.3 %all-reduce.3.cloned.1.call-done = bf16[32,1280]{1,0:T(8,128)(2,1)} async-done(((bf16[32,1280]{1,0:T(8,128)(2,1)}), bf16[32,1280]{1,0:T(8,128)(2,1)}) %all-reduce.3.cloned.1.call-update) | async-done | bytes 81936
  540.0 0.9 fusion.30
  540.9 0.9 multiply_reduce_fusion.4
  541.8 0.7 multiply_convert_fusion.2
  (72 shorter events, 2.5 us)
Async XLA Ops:
  7.2 39.1 %copy-start = (bf16[2,128,2560]{2,1,0:T(8,128)(2,1)S(1)}, bf16[2,128,2560]{2,1,0:T(8,128)(2,1)}, u32[]{:S(2)}) copy-start(bf16[2,128,2560]{2,1,0:T(8,128)(2,1)} %param.19) | copy-start | bytes 3932164
  11.9 35.5 %all-to-all-start = ((bf16[16,1,1]{2,1,0:T(2,128)(2,1)}), bf16[16,1,1]{2,1,0:T(2,128)(2,1)S(1)}, u32[]{:S(2)}, u32[]{:S(2)}) async-start(bf16[16,1,1]{2,1,0:T(2,128)(2,1)} %copy.91), calls=%async_computation | async-start | bytes 16384 | tf_op jit(solution)/shard_map/all_to_all | solution.py:99
  47.5 24.5 %all-to-all-start.1 = ((bf16[16,2,240]{2,1,0:T(2,128)(2,1)}), bf16[16,2,240]{2,1,0:T(2,128)(2,1)S(1)}, u32[]{:S(2)}, u32[]{:S(2)}) async-start(bf16[16,2,240]{2,1,0:T(2,128)(2,1)} %all_to_all.35), calls=%async_computation.1 | async-start | bytes 32768 | tf_op jit(solution)/shard_map/all_to_all | solution.py:31
  72.0 7.4 %copy-start.4 = (f32[1280]{0:T(1024)S(1)}, f32[1280]{0:T(1024)}, u32[]{:S(2)}) copy-start(f32[1280]{0:T(1024)} %param.31) | copy-start | bytes 15364
  72.0 8.1 %copy-start.7 = (s32[1,2]{1,0:T(1,128)S(1)}, s32[1,2]{1,0:T(1,128)}, u32[]{:S(2)}) copy-start(s32[1,2]{1,0:T(1,128)} %param.24) | copy-start | bytes 28
  72.0 235.0 %all-to-all-start.2 = ((bf16[16,128,2560]{2,1,0:T(8,128)(2,1)}), bf16[16,128,2560]{2,1,0:T(8,128)(2,1)}, u32[]{:S(2)}, u32[]{:S(2)}) async-start(bf16[16,128,2560]{2,1,0:T(8,128)(2,1)} %copy.94), calls=%async_computation.2 | async-start | bytes 20971520 | tf_op jit(solution)/shard_map/all_to_all | solution.py:98
  361.0 52.2 %copy-start.6 = (f32[320]{0:T(512)S(1)}, f32[320]{0:T(512)}, u32[]{:S(2)}) copy-start(f32[320]{0:T(512)} %param.35) | copy-start | bytes 3844
  362.9 58.0 %copy-start.2 = (bf16[2,1280]{1,0:T(2,128)(2,1)S(1)}, bf16[2,1280]{1,0:T(2,128)(2,1)}, u32[]{:S(2)}) copy-start(bf16[2,1280]{1,0:T(2,128)(2,1)} %param.18) | copy-start | bytes 15364
  362.9 58.0 %copy-start.3 = (f32[1280]{0:T(1024)S(1)}, f32[1280]{0:T(1024)}, u32[]{:S(2)}) copy-start(f32[1280]{0:T(1024)} %param.32) | copy-start | bytes 15364
  364.4 83.3 %copy-start.1 = (bf16[320,1280]{1,0:T(8,128)(2,1)S(1)}, bf16[320,1280]{1,0:T(8,128)(2,1)}, u32[]{:S(2)}) copy-start(bf16[320,1280]{1,0:T(8,128)(2,1)} %param.30) | copy-start | bytes 2457604
  408.6 12.0 %all-to-all-start.3 = ((bf16[16,2,80]{2,1,0:T(2,128)(2,1)}), bf16[16,2,80]{2,1,0:T(2,128)(2,1)S(1)}, u32[]{:S(2)}, u32[]{:S(2)}) async-start(bf16[16,2,80]{2,1,0:T(2,128)(2,1)} %bitcast.27), calls=%async_computation.3 | async-start | bytes 16384 | tf_op jit(solution)/shard_map/all_to_all | solution.py:31
  413.1 126.9 %all-reduce.3.cloned.1.call-start = ((), (), s32[]{:S(2)}) async-start(), calls=%async_computation.4 | async-start | bytes 163840
  445.6 4.7 copy-start.8
  451.5 89.3 %copy-start.5 = (f32[1280]{0:T(1024)S(1)}, f32[1280]{0:T(1024)}, u32[]{:S(2)}) copy-start(f32[1280]{0:T(1024)} %param.33) | copy-start | bytes 15364
Sparse Core Ops, SparseCore 0:
  450.4 89.5 all-reduce.2
where the time goes:
time: 550 us; the launch traced here: 549 us
  waiting for transfers between devices  320 us (58%)
  blocking collectives  120 us (22%)
  matrix products  33.4 us (6%)
  local copies, waits for them, and re-layouts  26.5 us (5%)
  starting transfers between devices  25.2 us (5%)
  between operations  15.6 us (3%)
  other arithmetic  8.59 us (2%)
    all_to_all x1, waiting for transfers between devices, per_device(): lax.all_to_all(outgoing, 'group', split_axis=0, concat_axis=0, tiled=True)  226 us
    unnamed x2, waiting for transfers between devices  87.3 us
    all_gather x2, blocking collectives, spread_columns(): lax.all_gather(row_block, 'shard', axis=0, tiled=True)  49.7 us
    all_gather x1, blocking collectives, per_device(): shard_rows = lax.all_gather(mixed_low, 'shard', axis=0, tiled=True)  23.5 us
    all_gather x1, blocking collectives, per_device(): lax.all_gather(last_high, 'group', axis=0, tiled=True)  15.7 us
    dot_general x1, matrix products, per_device(): jnp.einsum('jp,prc->jrc', picker, incoming, preferred_element_type=jnp.fl...  15.7 us
    all_gather x1, blocking collectives, per_device(): lax.all_gather(last_sum, 'group', axis=0, tiled=True)  15.6 us
    all_gather x1, blocking collectives, per_device(): lax.all_gather(last_weighted, 'group', axis=0, tiled=True)  15.2 us
  transfers between devices with their start and end apart: 5, of which 3 were waited for; matrix products, arithmetic and copies ran while one was open for 5% of the time, Pallas kernels for 0%

commit v1 on v0

--- a/solution.py
+++ b/solution.py
@@ -28,7 +28,12 @@
         weight,
         preferred_element_type=jnp.float32,
     ).astype(jnp.bfloat16)
-    return lax.all_to_all(columns, "shard", split_axis=0, concat_axis=1, tiled=True)
+    return jnp.concatenate(
+        lax.all_to_all(
+            jnp.stack(jnp.split(columns, lax.axis_size("shard"), axis=0)), "shard", 0, 0
+        ),
+        axis=1,
+    )
 
 
 def compact_local(kv_cache, keep_list, lengths, merge_index, merge_table):

time: 550 us -> 566 us (1.029)
  local copies, waits for them, and re-layouts: 26.5 us -> 43.3 us
    unnamed x25 -> x55, local copies, waits for them, and re-layouts: 3.71 us -> 20 us
  transfers between devices with their start and end apart: 5 -> 5, of which waited for: 3 -> 3; matrix products, arithmetic and copies ran while one was open for 5% -> 6% of each run, Pallas kernels for 0% -> 0%
where the time goes in v1:
time: 566 us; the launch traced here: 565 us
  waiting for transfers between devices  320 us (57%)
  blocking collectives  120 us (21%)
  local copies, waits for them, and re-layouts  43.3 us (8%)
  matrix products  32.7 us (6%)
  starting transfers between devices  25.3 us (4%)
  between operations  15.6 us (3%)
  other arithmetic  8.59 us (2%)
    all_to_all x1, waiting for transfers between devices, per_device(): lax.all_to_all(outgoing, 'group', split_axis=0, concat_axis=0, tiled=True)  226 us
    unnamed x2, waiting for transfers between devices  87.2 us
    all_gather x2, blocking collectives, spread_columns(): lax.all_gather(row_block, 'shard', axis=0, tiled=True)  49.7 us
    all_gather x1, blocking collectives, per_device(): shard_rows = lax.all_gather(mixed_low, 'shard', axis=0, tiled=True)  23.5 us
    unnamed x55, local copies, waits for them, and re-layouts  20 us
    all_gather x1, blocking collectives, per_device(): lax.all_gather(last_high, 'group', axis=0, tiled=True)  15.7 us
    dot_general x1, matrix products, per_device(): jnp.einsum('jp,prc->jrc', picker, incoming, preferred_element_type=jnp.fl...  15.7 us
    all_gather x1, blocking collectives, per_device(): lax.all_gather(last_sum, 'group', axis=0, tiled=True)  15.6 us
  transfers between devices with their start and end apart: 5, of which 3 were waited for; matrix products, arithmetic and copies ran while one was open for 6% of the time, Pallas kernels for 0%

profile of v1, /device:TPU:32, one launch (start us, length us, event | category | flops | bytes accessed | tf_op | source)
XLA Modules:
  0.0 565.3 jit_solution(8652213267616228055)
XLA Ops:
  7.2 0.8 convert_element_type.140
  7.9 0.8 select_reduce_fusion.1
  8.7 0.8 fusion.64
  9.5 0.8 broadcast_select_fusion
  10.2 0.7 fusion.43
  11.2 0.7 copy.90
  11.9 8.6 %all-to-all-start = ((bf16[16,1,1]{2,1,0:T(2,128)(2,1)}), bf16[16,1,1]{2,1,0:T(2,128)(2,1)S(1)}, u32[]{:S(2)}, u32[]{:S(2)}) async-start(bf16[16,1,1]{2,1,0:T(2,128)(2,1)} %copy.90), calls=%async_computation | async-start | bytes 16384 | tf_op jit(solution)/shard_map/all_to_all | solution.py:104
  20.9 23.9 %all-gather = bf16[16,2,1280]{2,1,0:T(2,128)(2,1)S(1)} all-gather(bf16[1,2,1280]{2,1,0:T(2,128)(2,1)} %bitcast.226), channel_id=1, replica_groups=mesh['group'=16,'shard'=16] {'shard'}, dimensions={0}, use_global_device_ids=true | all-gather | bytes 87040 | tf_op jit(solution)/shard_map/all_gather | solution.py:27
  44.9 1.3 convolution_convert_fusion.3
  46.2 0.6 constant_dynamic-update-slice_fusion.15
  46.8 0.6 constant_dynamic-update-slice_fusion.14
  49.1 0.6 constant_dynamic-update-slice_fusion.10
  49.7 0.6 constant_dynamic-update-slice_fusion.9
  50.2 0.6 constant_dynamic-update-slice_fusion.8
  51.4 0.6 constant_dynamic-update-slice_fusion.6
  53.6 0.6 constant_dynamic-update-slice_fusion.2
  54.2 0.6 constant_dynamic-update-slice_fusion.1
  55.3 0.6 constant_dynamic-update-slice_fusion
  55.9 4.7 all-to-all-start.1
  60.6 6.1 %convolution_convert_fusion = bf16[16,128,2560]{2,0,1:T(8,128)(2,1)} fusion(bf16[2,128,2560]{2,1,0:T(8,128)(2,1)S(1)} %convolution_convert_fusion.1, s32[2]{0:T(128)S(1)} %fusion.43), kind=kOutput, calls=%fused_computation.2 | convolution fusion | flops 26214432 | bytes 11796488 | tf_op jit(solution)/shard_map/pj,jrc->prc/dot_general | solution.py:96
  66.7 13.7 %copy.93 = bf16[16,128,2560]{2,1,0:T(8,128)(2,1)} copy(bf16[16,128,2560]{2,0,1:T(8,128)(2,1)} %convolution_convert_fusion) | data formatting | bytes 20971520 | tf_op jit(solution)/shard_map/convert_element_type | solution.py:96
  80.4 7.4 %all-to-all-start.2 = ((bf16[16,128,2560]{2,1,0:T(8,128)(2,1)}), bf16[16,128,2560]{2,1,0:T(8,128)(2,1)}, u32[]{:S(2)}, u32[]{:S(2)}) async-start(bf16[16,128,2560]{2,1,0:T(8,128)(2,1)} %copy.93), calls=%async_computation.2 | async-start | bytes 20971520 | tf_op jit(solution)/shard_map/all_to_all | solution.py:103
  89.8 225.6 %all-to-all-done.2 = bf16[16,128,2560]{2,1,0:T(8,128)(2,1)} async-done(((bf16[16,128,2560]{2,1,0:T(8,128)(2,1)}), bf16[16,128,2560]{2,1,0:T(8,128)(2,1)}, u32[]{:S(2)}, u32[]{:S(2)}) %all-to-all-start.2) | async-done | bytes 10485792 | tf_op jit(solution)/shard_map/all_to_all | solution.py:103
  315.4 15.7 %fusion.2 = bf16[2,128,2560]{2,0,1:T(2,128)(2,1)S(1)} fusion(bf16[16,128,2560]{2,1,0:T(8,128)(2,1)} %all-to-all-done.2, s32[2]{0:T(128)S(1)} %and_select_fusion.1), kind=kOutput, calls=%fused_computation.3 | convolution fusion | flops 21626912 | bytes 11796488 | tf_op jit(solution)/shard_map/jp,prc->jrc/dot_general | solution.py:110
  331.1 1.7 fusion.65
  332.8 3.0 copy.95
  335.8 1.4 fusion.25
  337.5 15.7 %all-gather.1 = f32[16,1,20]{2,1,0:T(1,128)S(1)} all-gather(f32[1,1,20]{2,1,0:T(1,128)S(1)} %slice_bitcast_fusion.33), channel_id=1, replica_groups=mesh['group'=16,'shard'=16] {'group'}, dimensions={0}, use_global_device_ids=true | all-gather | bytes 1360 | tf_op jit(solution)/shard_map/all_gather | solution.py:161
  353.6 15.6 %all-gather.2 = f32[16,1,20]{2,1,0:T(1,128)S(1)} all-gather(f32[1,1,20]{2,1,0:T(1,128)S(1)} %slice_bitcast_fusion.32), channel_id=1, replica_groups=mesh['group'=16,'shard'=16] {'group'}, dimensions={0}, use_global_device_ids=true | all-gather | bytes 1360 | tf_op jit(solution)/shard_map/all_gather | solution.py:162
  369.4 1.9 copy.98
  371.3 1.5 fusion.23
  372.9 15.2 %all_gather.20 = f32[16,20,64]{2,1,0:T(8,128)S(1)} all-gather(f32[1,20,64]{2,1,0:T(8,128)S(1)} %slice.46), channel_id=1, replica_groups=mesh['group'=16,'shard'=16] {'group'}, dimensions={0}, use_global_device_ids=true | all-gather | bytes 87040 | tf_op jit(solution)/shard_map/all_gather | solution.py:163
  388.5 25.7 %all-gather.3 = bf16[16,2,1280]{2,1,0:T(2,128)(2,1)} all-gather(bf16[1,2,1280]{2,1,0:T(2,128)(2,1)S(1)} %fusion.36), channel_id=1, replica_groups=mesh['group'=16,'shard'=16] {'shard'}, dimensions={0}, use_global_device_ids=true | all-gather | bytes 87040 | tf_op jit(solution)/shard_map/all_gather | solution.py:27
  414.3 0.9 reshape.288
  415.2 1.1 convolution_convert_fusion.4
  416.3 0.6 constant_dynamic-update-slice_fusion.31
  424.6 4.6 all-to-all-start.3
  429.3 7.4 %all-to-all-done.3 = bf16[16,2,80]{2,1,0:T(2,128)(2,1)S(1)} async-done(((bf16[16,2,80]{2,1,0:T(2,128)(2,1)}), bf16[16,2,80]{2,1,0:T(2,128)(2,1)S(1)}, u32[]{:S(2)}, u32[]{:S(2)}) %all-to-all-start.3) | async-done | bytes 5152 | tf_op jit(solution)/shard_map/all_to_all | solution.py:32
  437.2 23.5 %all-gather.4 = bf16[16,2,1280]{2,1,0:T(2,128)(2,1)} all-gather(bf16[1,2,1280]{2,1,0:T(2,128)(2,1)S(1)} %fusion.35), channel_id=1, replica_groups=mesh['group'=16,'shard'=16] {'shard'}, dimensions={0}, use_global_device_ids=true | all-gather | bytes 87040 | tf_op jit(solution)/shard_map/all_gather | solution.py:188
  460.7 0.9 reshape.290
  461.6 2.1 convolution_multiply_fusion
  463.8 2.6 convolution_convert_fusion.2
  466.4 0.6 dynamic-slice
  467.6 1.2 copy.101
  468.8 87.2 %all-reduce.3.cloned.1.call-done = bf16[32,1280]{1,0:T(8,128)(2,1)} async-done(((bf16[32,1280]{1,0:T(8,128)(2,1)}), bf16[32,1280]{1,0:T(8,128)(2,1)}) %all-reduce.3.cloned.1.call-update) | async-done | bytes 81936
  556.0 0.9 fusion.30
  556.9 0.9 multiply_reduce_fusion.4
  557.8 0.7 multiply_convert_fusion.2
  (103 shorter events, 16.3 us)
Async XLA Ops:
  7.2 47.6 %copy-start = (bf16[2,128,2560]{2,1,0:T(8,128)(2,1)S(1)}, bf16[2,128,2560]{2,1,0:T(8,128)(2,1)}, u32[]{:S(2)}) copy-start(bf16[2,128,2560]{2,1,0:T(8,128)(2,1)} %param.19) | copy-start | bytes 3932164
  11.9 44.0 %all-to-all-start = ((bf16[16,1,1]{2,1,0:T(2,128)(2,1)}), bf16[16,1,1]{2,1,0:T(2,128)(2,1)S(1)}, u32[]{:S(2)}, u32[]{:S(2)}) async-start(bf16[16,1,1]{2,1,0:T(2,128)(2,1)} %copy.90), calls=%async_computation | async-start | bytes 16384 | tf_op jit(solution)/shard_map/all_to_all | solution.py:104
  55.9 24.5 %all-to-all-start.1 = ((bf16[16,2,240]{2,1,0:T(2,128)(2,1)}), bf16[16,2,240]{2,1,0:T(2,128)(2,1)S(1)}, u32[]{:S(2)}, u32[]{:S(2)}) async-start(bf16[16,2,240]{2,1,0:T(2,128)(2,1)} %constant_dynamic-update-slice_fusion), calls=%async_computation.1 | async-start | bytes 32768 | tf_op jit(solution)/shard_map/all_to_all | solution.py:32
  80.4 7.4 %copy-start.4 = (f32[1280]{0:T(1024)S(1)}, f32[1280]{0:T(1024)}, u32[]{:S(2)}) copy-start(f32[1280]{0:T(1024)} %param.31) | copy-start | bytes 15364
  80.4 8.2 %copy-start.7 = (s32[1,2]{1,0:T(1,128)S(1)}, s32[1,2]{1,0:T(1,128)}, u32[]{:S(2)}) copy-start(s32[1,2]{1,0:T(1,128)} %param.24) | copy-start | bytes 28
  80.4 235.0 %all-to-all-start.2 = ((bf16[16,128,2560]{2,1,0:T(8,128)(2,1)}), bf16[16,128,2560]{2,1,0:T(8,128)(2,1)}, u32[]{:S(2)}, u32[]{:S(2)}) async-start(bf16[16,128,2560]{2,1,0:T(8,128)(2,1)} %copy.93), calls=%async_computation.2 | async-start | bytes 20971520 | tf_op jit(solution)/shard_map/all_to_all | solution.py:103
  369.4 59.8 %copy-start.6 = (f32[320]{0:T(512)S(1)}, f32[320]{0:T(512)}, u32[]{:S(2)}) copy-start(f32[320]{0:T(512)} %param.35) | copy-start | bytes 3844
  371.3 65.6 %copy-start.2 = (bf16[2,1280]{1,0:T(2,128)(2,1)S(1)}, bf16[2,1280]{1,0:T(2,128)(2,1)}, u32[]{:S(2)}) copy-start(bf16[2,1280]{1,0:T(2,128)(2,1)} %param.18) | copy-start | bytes 15364
  371.3 65.6 %copy-start.3 = (f32[1280]{0:T(1024)S(1)}, f32[1280]{0:T(1024)}, u32[]{:S(2)}) copy-start(f32[1280]{0:T(1024)} %param.32) | copy-start | bytes 15364
  372.9 90.9 %copy-start.1 = (bf16[320,1280]{1,0:T(8,128)(2,1)S(1)}, bf16[320,1280]{1,0:T(8,128)(2,1)}, u32[]{:S(2)}) copy-start(bf16[320,1280]{1,0:T(8,128)(2,1)} %param.30) | copy-start | bytes 2457604
  424.6 12.1 %all-to-all-start.3 = ((bf16[16,2,80]{2,1,0:T(2,128)(2,1)}), bf16[16,2,80]{2,1,0:T(2,128)(2,1)S(1)}, u32[]{:S(2)}, u32[]{:S(2)}) async-start(bf16[16,2,80]{2,1,0:T(2,128)(2,1)} %constant_dynamic-update-slice_fusion.16), calls=%async_computation.3 | async-start | bytes 16384 | tf_op jit(solution)/shard_map/all_to_all | solution.py:32
  429.2 126.8 %all-reduce.3.cloned.1.call-start = ((), (), s32[]{:S(2)}) async-start(), calls=%async_computation.4 | async-start | bytes 163840
  461.6 4.7 copy-start.8
  467.6 89.3 %copy-start.5 = (f32[1280]{0:T(1024)S(1)}, f32[1280]{0:T(1024)}, u32[]{:S(2)}) copy-start(f32[1280]{0:T(1024)} %param.33) | copy-start | bytes 15364
Sparse Core Ops, SparseCore 0:
  466.5 89.4 all-reduce.2
